TPU v7x, 32 devices: a whole 2x2x4 slice. The times are simulated.
32 devices in a mesh: seq: 4 (over x, core), dp: 8 (over z, y).
Axes of the slice: x: 2, y: 2, z: 4, core: 2. Of those that a mesh axis runs over, the one named last changes fastest.
Arguments:
- inputs: bfloat16 [8, 1024, 4096], P('dp', 'seq'), may hold values from -6 to 6
- queries: bfloat16 [8, 1024, 256], P('dp', 'seq'), may hold values from -6 to 6
- keys: bfloat16 [8, 1024, 256], P('dp', 'seq'), may hold values from -6 to 6
- values: bfloat16 [8, 1024, 256], P('dp', 'seq'), may hold values from -6 to 6
- out_grad: bfloat16 [8, 1024, 256], P('dp', 'seq'), may hold values from -6 to 6
Outputs:
- qkv_grad: bfloat16 [8, 1024, 768], P('dp', 'seq')
- weight_grad: float32 [4096, 768], P('dp')
All inputs are finite; a program needn't handle non-finite values.
Results may differ from a plain program's by a relative error of at most 0.014.
Values may be sent and summed in bfloat16 or wider, within the bound.
No kernel may reach another device: no remote copies, remote signals or barrier semaphores. Data moves between devices by JAX's collectives and lax.ppermute only.
A program may use at most 64 MiB of HBM per device.

v0:
```python
import jax
import jax.numpy as jnp
from jax import lax
from jax.sharding import PartitionSpec as P

HS = 128
HEADS = 2


def block_grads(query, key, value, grad_out, prefix, suffix, scale):
    count = query.shape[0]
    causal = jnp.arange(count)[:, None] >= jnp.arange(count)[None, :]
    f32 = jnp.float32
    score_a = jnp.einsum("thd,shd->hts", grad_out, value, preferred_element_type=f32)
    score_a = jnp.where(causal[None], score_a, 0.0).astype(jnp.bfloat16)
    score_b = jnp.einsum("thd,shd->hts", query, key, preferred_element_type=f32)
    score_b = jnp.where(causal[None], score_b, 0.0).astype(jnp.bfloat16)
    grad_q = jnp.einsum("hts,shd->thd", score_a, key, preferred_element_type=f32) + jnp.einsum(
        "thb,hab->tha", grad_out, prefix, preferred_element_type=f32
    )
    grad_k = jnp.einsum("htj,thd->jhd", score_a, query, preferred_element_type=f32) + jnp.einsum(
        "jhb,hab->jha", value, suffix, preferred_element_type=f32
    )
    grad_v = jnp.einsum("htj,thd->jhd", score_b, grad_out, preferred_element_type=f32) + jnp.einsum(
        "jha,hab->jhb", key, suffix, preferred_element_type=f32
    )
    joined = jnp.concatenate([grad_q, grad_k, grad_v], axis=1) * scale
    return joined.reshape(count, -1).astype(jnp.bfloat16)


def on_device(inputs, queries, keys, values, out_grad):
    tokens = queries.shape[1]
    seq_count = lax.axis_size("seq")
    batch_count = lax.axis_size("dp")
    length_all = tokens * seq_count
    scale = 1.0 / jnp.sqrt(jnp.float32(HS * length_all))
    weight_scale = 1.0 / jnp.sqrt(jnp.float32(batch_count * length_all))
    shape = (tokens, HEADS, HS)
    query = queries[0].reshape(shape)
    key = keys[0].reshape(shape)
    value = values[0].reshape(shape)
    grad_out = out_grad[0].reshape(shape)
    kv_state = jnp.einsum("lhi,lhj->hij", key, value, preferred_element_type=jnp.float32).astype(
        jnp.bfloat16
    )
    dq_state = jnp.einsum(
        "lhi,lhj->hij", query, grad_out, preferred_element_type=jnp.float32
    ).astype(jnp.bfloat16)
    stacked = jnp.stack([kv_state, dq_state])[None]
    position = lax.axis_index("seq")
    piece = lax.all_gather(stacked, "seq", axis=0, tiled=True)
    owners = jnp.arange(piece.shape[0])
    lower = (owners < position).astype(jnp.float32)
    higher = (owners > position).astype(jnp.float32)
    wide = piece.astype(jnp.float32)
    prefix = jnp.einsum("n,nhij->hij", lower, wide[:, 0])
    suffix = jnp.einsum("n,nhij->hij", higher, wide[:, 1])
    prefix = prefix.astype(jnp.bfloat16)
    suffix = suffix.astype(jnp.bfloat16)
    grads = block_grads(query, key, value, grad_out, prefix, suffix, scale)
    features = inputs[0]
    rows_here = lax.psum_scatter(
        (
            lax.dot_general(
                features, grads, (((0,), (0,)), ((), ())), preferred_element_type=jnp.float32
            )
            * weight_scale
        ).astype(jnp.bfloat16),
        "dp",
        scatter_dimension=0,
        tiled=True,
    )
    weight_grad = lax.psum(rows_here, "seq").astype(jnp.float32)
    return (grads[None], weight_grad)


def solution(mesh):
    in_specs = (
        P("dp", "seq", None),
        P("dp", "seq", None),
        P("dp", "seq", None),
        P("dp", "seq", None),
        P("dp", "seq", None),
    )
    out_specs = (P("dp", "seq", None), P("dp", None))
    return jax.shard_map(
        on_device, mesh=mesh, in_specs=in_specs, out_specs=out_specs, check_vma=False
    )
```

profile of v0, /device:TPU:0, one launch (start us, length us, event | category | flops | bytes accessed | tf_op | source)
XLA Modules:
  0.0 193.3 jit_solution(12286816662715219097)
XLA Ops:
  7.3 1.1 reshape_squeeze.14
  8.4 0.9 reshape_squeeze.15
  9.3 0.9 reshape_squeeze.13
  10.2 1.0 copy.45
  11.3 0.2 fusion.9
  11.5 0.2 fusion.10
  11.7 8.6 %all-gather = bf16[8,2,128,128]{3,2,1,0:T(8,128)(2,1)S(1)} all-gather(bf16[2,2,128,128]{3,2,1,0:T(8,128)(2,1)S(1)} %pad_maximum_fusion), channel_id=2, replica_groups=mesh['seq'=4,'dp'=8] {'seq'}, dimensions={0}, use_global_device_ids=true | all-gather | bytes 655360 | tf_op jit(solution)/shard_map/all_gather | solution.py:51
  20.4 0.3 fusion.13
  20.7 0.1 copy.42
  20.8 0.2 convolution_bitcast_fusion.3
  21.1 0.2 convolution_bitcast_fusion.2
  21.3 0.3 fusion.2
  21.5 0.3 fusion.15
  21.8 0.2 convolution_bitcast_fusion.4
  22.0 0.2 fusion.7
  22.3 0.2 fusion.6
  22.5 1.2 fusion.8
  23.7 0.1 fusion.11
  23.8 4.5 %fusion = bf16[4096,768]{0,1:T(8,128)(2,1)} fusion(bf16[256,768]{0,1:T(8,128)(2,1)S(1)} %bitcast.58, bf16[1,256,4096]{2,1,0:T(8,128)(2,1)S(1)} %copy-done), kind=kOutput, calls=%fused_computation.1 | convolution fusion | flops 1616904192 | bytes 8781824 | tf_op jit(solution)/shard_map/dot_general | solution.py:64
  28.3 0.0 all-reduce.2.cloned.1.call-start
  28.4 119.3 %reduce-scatter.2.cloned.1.call-done = bf16[512,768]{0,1:T(8,128)(2,1)} async-done(((bf16[4096,768]{0,1:T(8,128)(2,1)}), bf16[512,768]{0,1:T(8,128)(2,1)}) %reduce-scatter.2.cloned.1.call-update) | async-done | bytes 786448 | tf_op jit(solution)/shard_map/reduce_scatter | solution.py:62
  147.7 0.9 copy.35
  148.6 35.2 %all-reduce.2.cloned.1.call-done = bf16[512,768]{0,1:T(8,128)(2,1)} async-done(((bf16[512,768]{0,1:T(8,128)(2,1)}), bf16[512,768]{0,1:T(8,128)(2,1)}) %all-reduce.2.cloned.1.call-update) | async-done | bytes 786448 | tf_op jit(solution)/shard_map/psum | solution.py:73
  183.9 2.5 %copy.36 = f32[512,768]{1,0:T(8,128)} copy(bf16[512,768]{0,1:T(8,128)(2,1)} %all-reduce.2.cloned.1.call-done) | data formatting | bytes 2359296
  (10 shorter events, 0.2 us)
Async XLA Ops:
  7.2 16.7 %copy-start = (bf16[1,256,4096]{2,1,0:T(8,128)(2,1)S(1)}, bf16[1,256,4096]{2,1,0:T(8,128)(2,1)}, u32[]{:S(2)}) copy-start(bf16[1,256,4096]{2,1,0:T(8,128)(2,1)} %param.5) | copy-start | bytes 6291460
  7.2 140.5 %reduce-scatter.2.cloned.1.call-start = ((), (), s32[]{:S(2)}) async-start(), calls=%async_computation.1 | async-start | bytes 7077888 | tf_op jit(solution)/shard_map/reduce_scatter | solution.py:62
  7.3 14.7 %copy-start.1 = (pred[256,256]{1,0:T(8,128)(4,1)}, pred[256,256]{1,0:T(8,128)(4,1)S(1)}, u32[]{:S(2)}) copy-start(pred[256,256]{1,0:T(8,128)(4,1)S(1)} %iota_compare_fusion) | copy-start | bytes 196612
  28.3 155.6 %all-reduce.2.cloned.1.call-start = ((), (), s32[]{:S(2)}) async-start(), calls=%async_computation.2 | async-start | bytes 1572864 | tf_op jit(solution)/shard_map/psum | solution.py:73
Sparse Core Ops, SparseCore 0:
  28.4 119.2 reduce-scatter.1
  150.1 33.7 all-reduce.1
where the time goes:
time: 194 us; the launch traced here: 193 us
  waiting for transfers between devices  155 us (80%)
  between operations  14.2 us (7%)
  blocking collectives  8.62 us (4%)
  matrix products  8.03 us (4%)
  local copies, waits for them, and re-layouts  7.61 us (4%)
    reduce_scatter x1, waiting for transfers between devices, on_device(): lax.psum_scatter((lax.dot_general(features, grads, (((0,), (0,)), ((), ()...  119 us
    psum x1, waiting for transfers between devices, on_device(): weight_grad = lax.psum(rows_here, 'seq').astype(jnp.float32)  35.2 us
    all_gather x1, blocking collectives, on_device(): piece = lax.all_gather(stacked, 'seq', axis=0, tiled=True)  8.62 us
    dot_general x1, matrix products, on_device(): lax.dot_general(features, grads, (((0,), (0,)), ((), ())), preferred_elem...  4.45 us
  transfers between devices with their start and end apart: 2, of which 2 were waited for; matrix products, arithmetic and copies ran while one was open for 0% of the time, Pallas kernels for 0%

commit v1 on v0

--- a/solution.py
+++ b/solution.py
@@ -48,7 +48,12 @@
     ).astype(jnp.bfloat16)
     stacked = jnp.stack([kv_state, dq_state])[None]
     position = lax.axis_index("seq")
-    piece = lax.all_gather(stacked, "seq", axis=0, tiled=True)
+    ring = [stacked]
+    for hop in range(3):
+        ring.append(lax.ppermute(ring[-1], "seq", [(dev, (dev + 1) % 4) for dev in range(4)]))
+    piece = jnp.roll(
+        jnp.concatenate(ring[::-1], axis=0), (lax.axis_index("seq") + 1) * ring[0].shape[0], axis=0
+    )
     owners = jnp.arange(piece.shape[0])
     lower = (owners < position).astype(jnp.float32)
     higher = (owners > position).astype(jnp.float32)

time: 194 us -> 201 us (1.036)
  waiting for transfers between devices: 155 us -> 169 us
  blocking collectives: 8.62 us -> 0 us
    ppermute x0 -> x3, waiting for transfers between devices: none -> 13.1 us  [on_device(): lax.ppermute(ring[-1], 'seq', [(dev, (dev + 1) % 4) for dev in range(4)])]
    all_gather x1 -> x0, blocking collectives: 8.62 us -> none  [on_device(): piece = lax.all_gather(stacked, 'seq', axis=0, tiled=True)]
  transfers between devices with their start and end apart: 2 -> 5, of which waited for: 2 -> 5; matrix products, arithmetic and copies ran while one was open for 0% -> 1% of each run, Pallas kernels for 0% -> 0%
where the time goes in v1:
time: 201 us; the launch traced here: 200 us
  waiting for transfers between devices  169 us (84%)
  between operations  14.2 us (7%)
  matrix products  8.84 us (4%)
  local copies, waits for them, and re-layouts  7.73 us (4%)
    reduce_scatter x1, waiting for transfers between devices, on_device(): lax.psum_scatter((lax.dot_general(features, grads, (((0,), (0,)), ((), ()...  121 us
    psum x1, waiting for transfers between devices, on_device(): weight_grad = lax.psum(rows_here, 'seq').astype(jnp.float32)  35.2 us
    ppermute x3, waiting for transfers between devices, on_device(): lax.ppermute(ring[-1], 'seq', [(dev, (dev + 1) % 4) for dev in range(4)])  13.1 us
    dot_general x1, matrix products, on_device(): lax.dot_general(features, grads, (((0,), (0,)), ((), ())), preferred_elem...  4.46 us
  transfers between devices with their start and end apart: 5, of which 5 were waited for; matrix products, arithmetic and copies ran while one was open for 1% of the time, Pallas kernels for 0%

profile of v1, /device:TPU:0, one launch (start us, length us, event | category | flops | bytes accessed | tf_op | source)
XLA Modules:
  0.0 200.4 jit_solution(5762002566043930431)
XLA Ops:
  7.2 1.1 reshape_squeeze.14
  8.3 0.9 reshape_squeeze.15
  9.2 0.9 reshape_squeeze.13
  10.2 1.0 copy.30
  11.2 0.2 fusion.9
  11.4 0.2 fusion.10
  11.7 0.5 collective-permute-start
  12.2 4.6 %collective-permute-done = bf16[1,2,2,128,128]{4,3,2,1,0:T(8,128)(2,1)S(1)} collective-permute-done((bf16[1,2,2,128,128]{4,3,2,1,0:T(8,128)(2,1)S(1)}, bf16[1,2,2,128,128]{4,3,2,1,0:T(8,128)(2,1)S(1)}, u32[]{:S(2)}, u32[]{:S(2)}) %collective-permute-start) | collective-permute-done | bytes 131104 | tf_op jit(solution)/shard_map/ppermute | solution.py:53
  16.8 4.4 %collective-permute-done.1 = bf16[1,2,2,128,128]{4,3,2,1,0:T(8,128)(2,1)S(1)} collective-permute-done((bf16[1,2,2,128,128]{4,3,2,1,0:T(8,128)(2,1)S(1)}, bf16[1,2,2,128,128]{4,3,2,1,0:T(8,128)(2,1)S(1)}, u32[]{:S(2)}, u32[]{:S(2)}) %collective-permute-start.1) | collective-permute-done | bytes 131104 | tf_op jit(solution)/shard_map/ppermute | solution.py:53
  21.2 0.3 fusion.2
  21.4 4.1 %collective-permute-done.2 = bf16[1,2,2,128,128]{4,3,2,1,0:T(8,128)(2,1)S(1)} collective-permute-done((bf16[1,2,2,128,128]{4,3,2,1,0:T(8,128)(2,1)S(1)}, bf16[1,2,2,128,128]{4,3,2,1,0:T(8,128)(2,1)S(1)}, u32[]{:S(2)}, u32[]{:S(2)}) %collective-permute-start.2) | collective-permute-done | bytes 131104 | tf_op jit(solution)/shard_map/ppermute | solution.py:53
  25.8 0.3 fusion.13
  26.2 0.2 convolution_bitcast_fusion.3
  26.5 0.9 convolution_bitcast_fusion.2
  27.4 0.3 fusion.15
  27.7 0.2 convolution_bitcast_fusion.4
  27.8 0.2 fusion.7
  28.1 0.2 fusion.6
  28.3 1.3 fusion.8
  29.8 4.5 %fusion = bf16[4096,768]{0,1:T(8,128)(2,1)} fusion(bf16[256,768]{0,1:T(8,128)(2,1)S(1)} %bitcast.63, bf16[1,256,4096]{2,1,0:T(8,128)(2,1)S(1)} %copy-done), kind=kOutput, calls=%fused_computation.1 | convolution fusion | flops 1616904192 | bytes 8781824 | tf_op jit(solution)/shard_map/dot_general | solution.py:69
  34.3 120.5 %reduce-scatter.2.cloned.1.call-done = bf16[512,768]{0,1:T(8,128)(2,1)} async-done(((bf16[4096,768]{0,1:T(8,128)(2,1)}), bf16[512,768]{0,1:T(8,128)(2,1)}) %reduce-scatter.2.cloned.1.call-update) | async-done | bytes 786448 | tf_op jit(solution)/shard_map/reduce_scatter | solution.py:67
  154.8 0.9 copy.20
  155.8 35.2 %all-reduce.2.cloned.1.call-done = bf16[512,768]{0,1:T(8,128)(2,1)} async-done(((bf16[512,768]{0,1:T(8,128)(2,1)}), bf16[512,768]{0,1:T(8,128)(2,1)}) %all-reduce.2.cloned.1.call-update) | async-done | bytes 786448 | tf_op jit(solution)/shard_map/psum | solution.py:78
  191.0 2.5 %copy.21 = f32[512,768]{1,0:T(8,128)} copy(bf16[512,768]{0,1:T(8,128)(2,1)} %all-reduce.2.cloned.1.call-done) | data formatting | bytes 2359296
  (21 shorter events, 0.6 us)
Async XLA Ops:
  7.2 22.6 %copy-start = (bf16[1,256,4096]{2,1,0:T(8,128)(2,1)S(1)}, bf16[1,256,4096]{2,1,0:T(8,128)(2,1)}, u32[]{:S(2)}) copy-start(bf16[1,256,4096]{2,1,0:T(8,128)(2,1)} %param.5) | copy-start | bytes 6291460
  7.2 147.6 %reduce-scatter.2.cloned.1.call-start = ((), (), s32[]{:S(2)}) async-start(), calls=%async_computation.1 | async-start | bytes 7077888 | tf_op jit(solution)/shard_map/reduce_scatter | solution.py:67
  11.7 5.1 %collective-permute-start = (bf16[1,2,2,128,128]{4,3,2,1,0:T(8,128)(2,1)S(1)}, bf16[1,2,2,128,128]{4,3,2,1,0:T(8,128)(2,1)S(1)}, u32[]{:S(2)}, u32[]{:S(2)}) collective-permute-start(bf16[1,2,2,128,128]{4,3,2,1,0:T(8,128)(2,1)S(1)} %maximum_bitcast_fusion), channel_id=1, source_target_pairs={{0,8},{8,16},{16,24},{24,0},{1,9},{9,17},{17,25},{25,1},{2,10},{10... | collective-permute-start | bytes 393224 | tf_op jit(solution)/shard_map/ppermute | solution.py:53
  16.8 4.4 %collective-permute-start.1 = (bf16[1,2,2,128,128]{4,3,2,1,0:T(8,128)(2,1)S(1)}, bf16[1,2,2,128,128]{4,3,2,1,0:T(8,128)(2,1)S(1)}, u32[]{:S(2)}, u32[]{:S(2)}) collective-permute-start(bf16[1,2,2,128,128]{4,3,2,1,0:T(8,128)(2,1)S(1)} %collective-permute-done), channel_id=1, source_target_pairs={{0,8},{8,16},{16,24},{24,0},{1,9},{9,17},{17,25},{25,1},{2,10},{10... | collective-permute-start | bytes 393224 | tf_op jit(solution)/shard_map/ppermute | solution.py:53
  21.2 4.4 %collective-permute-start.2 = (bf16[1,2,2,128,128]{4,3,2,1,0:T(8,128)(2,1)S(1)}, bf16[1,2,2,128,128]{4,3,2,1,0:T(8,128)(2,1)S(1)}, u32[]{:S(2)}, u32[]{:S(2)}) collective-permute-start(bf16[1,2,2,128,128]{4,3,2,1,0:T(8,128)(2,1)S(1)} %collective-permute-done.1), channel_id=1, source_target_pairs={{0,8},{8,16},{16,24},{24,0},{1,9},{9,17},{17,25},{25,1},{2,10},{10... | collective-permute-start | bytes 393224 | tf_op jit(solution)/shard_map/ppermute | solution.py:53
  34.2 156.8 %all-reduce.2.cloned.1.call-start = ((), (), s32[]{:S(2)}) async-start(), calls=%async_computation.2 | async-start | bytes 1572864 | tf_op jit(solution)/shard_map/psum | solution.py:78
Sparse Core Ops, SparseCore 0:
  34.4 120.4 reduce-scatter.1
  157.2 33.7 all-reduce.1
